TPU v7x, 128 devices: a whole 4x4x4 slice. The times are simulated.
128 devices in a mesh: rows: 16 (over z_lo, x, core), batch: 8 (over z_hi, y).
Axes of the slice: x: 4, y: 4, z: 4 (z_hi: 2, z_lo: 2; z = z_hi * 2 + z_lo), core: 2. Of those that a mesh axis runs over, the one named last changes fastest.
Arguments:
- bases: bfloat16 [49152, 2048], P('rows', 'batch'), may hold values from -30 to 30
- start: float32 [2048, 512], P('batch'), may hold values from -6 to 6
Outputs:
- modes: bfloat16 [49152, 512], P(('rows', 'batch'))
All inputs are finite; a program needn't handle non-finite values.
Results may differ from a plain program's by a relative error of at most 0.0041.
Values may be sent and summed in bfloat16 or wider, within the bound.
A program may use at most 128 MiB of HBM per device.

v0:
```python
import jax
import jax.numpy as jnp
from jax import lax
from jax.sharding import PartitionSpec as P

ITERS = 2


def inner_cols(left, right):
    return lax.dot_general(
        left, right, (((0,), (0,)), ((), ())), preferred_element_type=jnp.float32
    )


def on_device(bases, start):
    basis_width = bases.shape[1]
    group_count = lax.axis_size("batch")
    all_columns = basis_width * group_count
    energy = lax.psum(jnp.sum(jnp.square(bases.astype(jnp.float32))), ("rows", "batch"))
    diag_mean = energy / all_columns
    partial_value = inner_cols(bases, lax.all_gather(bases, "batch", axis=1, tiled=True))
    gram_rows = lax.psum(partial_value, "rows")
    q_own = start
    for iteration in range(ITERS):
        q_full = lax.all_gather(q_own, "batch", axis=0, tiled=True)
        lifted = jnp.dot(gram_rows, q_full, precision=lax.Precision.HIGHEST) / diag_mean + q_own
        local_correlation = lax.dot_general(
            lifted, lifted, (((0,), (0,)), ((), ())), precision=lax.Precision.HIGHEST
        )
        correlation = lax.psum(local_correlation, "batch")
        factor = jnp.linalg.cholesky(correlation)
        q_own = jax.scipy.linalg.solve_triangular(factor, lifted.T, lower=True).T
    q_low = q_own.astype(jnp.bfloat16)
    modes = lax.psum_scatter(
        jnp.dot(bases, q_low, preferred_element_type=jnp.float32),
        "batch",
        scatter_dimension=0,
        tiled=True,
    )
    return modes.astype(jnp.bfloat16)


def solution(mesh):
    in_specs = (P("rows", "batch"), P("batch", None))
    out_specs = P(("rows", "batch"), None)
    return jax.shard_map(
        on_device, mesh=mesh, in_specs=in_specs, out_specs=out_specs, check_vma=False
    )
```

profile of v0, /device:TPU:0, one launch (start us, length us, event | category | flops | bytes accessed | tf_op | source)
XLA Modules:
  0.0 1044.4 jit_solution(2930456255555356268)
XLA Ops:
  8.1 166.4 %all-gather.4.cloned.1.call-done = bf16[3072,2048]{1,0:T(8,128)(2,1)} async-done(((bf16[3072,256]{1,0:T(8,128)(2,1)}), bf16[3072,2048]{1,0:T(8,128)(2,1)}) %all-gather.4.cloned.1.call-update) | async-done | bytes 12582928 | tf_op jit(solution)/shard_map/all_gather | solution.py:21
  174.4 7.8 fusion.76
  182.3 1.4 multiply_reduce_fusion
  183.7 78.1 %psum.29 = f32[]{:T(128)} all-reduce(f32[]{:T(128)} %multiply_reduce_fusion), channel_id=1, replica_groups=mesh['rows'=16,'batch'=8] {'rows','batch'}, use_global_device_ids=true, to_apply=%region_2.0 | all-reduce | flops 1 | bytes 8 | tf_op jit(solution)/shard_map/psum | solution.py:19
  262.5 108.6 %all-reduce.5.cloned.1.call-done = f32[256,2048]{1,0:T(8,128)} async-done(((f32[256,2048]{1,0:T(8,128)}), f32[256,2048]{1,0:T(8,128)}) %all-reduce.5.cloned.1.call-update) | async-done | bytes 2097168 | tf_op jit(solution)/shard_map/psum | solution.py:22
  371.1 6.2 fusion
  377.3 2.1 fusion.77
  379.9 88.5 %all-reduce.7.cloned.1.call-done = f32[512,512]{0,1:T(8,128)} async-done(((f32[512,512]{0,1:T(8,128)}), f32[512,512]{0,1:T(8,128)}) %all-reduce.7.cloned.1.call-update) | async-done | bytes 1048592 | tf_op jit(solution)/shard_map/psum | solution.py:30
  468.5 2.7 copy.4
  471.2 1.4 fusion.2
  473.6 11.7 %cholesky.286 = f32[128,128]{1,0:T(8,128)S(1)} custom-call(f32[128,128]{1,0:T(8,128)S(1)} %cholesky.426), custom_call_target="Cholesky" | custom-call | tf_op jit(solution)/shard_map/jit(cholesky)/cholesky | solution.py:31
  485.4 9.8 custom-call.27
  497.8 11.7 %cholesky.305 = f32[128,128]{1,0:T(8,128)S(1)} custom-call(f32[128,128]{1,0:T(8,128)S(1)} %cholesky.430), custom_call_target="Cholesky" | custom-call | tf_op jit(solution)/shard_map/jit(cholesky)/cholesky | solution.py:31
  509.6 10.0 custom-call.28
  521.1 11.7 %cholesky.326 = f32[128,128]{1,0:T(8,128)S(1)} custom-call(f32[128,128]{1,0:T(8,128)S(1)} %cholesky.435), custom_call_target="Cholesky" | custom-call | tf_op jit(solution)/shard_map/jit(cholesky)/cholesky | solution.py:31
  533.6 9.8 custom-call.29
  544.8 11.7 %cholesky.343 = f32[128,128]{1,0:T(8,128)S(1)} custom-call(f32[128,128]{1,0:T(8,128)S(1)} %convolution_subtract_fusion.11), custom_call_target="Cholesky" | custom-call | tf_op jit(solution)/shard_map/jit(cholesky)/cholesky | solution.py:31
  561.8 11.7 %while.4 = (s32[]{:T(128)}, f32[512,512]{1,0:T(8,128)}, s32[4,2]{0,1:T(2,128)S(1)}, f32[4,128,128]{2,1,0:T(8,128)S(1)}, s32[]{:T(128)}) while((s32[]{:T(128)}, f32[512,512]{1,0:T(8,128)}, s32[4,2]{0,1:T(2,128)S(1)}, f32[4,128,128]{2,1,0:T(8,128)S(1)}, s32[]{:T(128)}) %tuple.52), condition=%wide.while_cond, body=%wide.while_body.sunk | while | flops 2 | bytes 131181 | solution.py:32
  562.5 2.3 bitcast_dynamic-update-slice_fusion.4
  565.4 2.3 bitcast_dynamic-update-slice_fusion.4
  568.4 2.3 bitcast_dynamic-update-slice_fusion.4
  571.3 2.2 bitcast_dynamic-update-slice_fusion.4
  573.5 39.3 %custom-call.30 = f32[4,128,128]{1,2,0:T(8,128)S(1)} custom-call(f32[4,128,128]{2,1,0:T(8,128)S(1)} %get-tuple-element.21), custom_call_target="InvertDiagBlocksLowerTriangular" | custom-call | tf_op jit(solution)/shard_map/jit(_solve_triangular)/triangular_solve | solution.py:32
  614.7 1.5 convolution_subtract_fusion.6
  616.5 1.7 convolution_subtract_fusion.5
  619.7 69.7 %all-gather.8.cloned.1.call-done = f32[2048,512]{1,0:T(8,128)} async-done(((f32[256,512]{1,0:T(8,128)}), f32[2048,512]{1,0:T(8,128)}) %all-gather.8.cloned.1.call-update) | async-done | bytes 4194320 | tf_op jit(solution)/shard_map/all_gather | solution.py:25
  689.4 6.3 bitcast_add_fusion.2
  695.7 2.1 fusion.3
  698.3 85.3 %all-reduce.9.cloned.1.call-done = f32[512,512]{0,1:T(8,128)} async-done(((f32[512,512]{0,1:T(8,128)}), f32[512,512]{0,1:T(8,128)}) %all-reduce.9.cloned.1.call-update) | async-done | bytes 1048592 | tf_op jit(solution)/shard_map/psum | solution.py:30
  783.7 2.7 copy.10
  786.4 1.4 fusion.1
  788.8 11.7 %cholesky.358 = f32[128,128]{1,0:T(8,128)S(1)} custom-call(f32[128,128]{1,0:T(8,128)S(1)} %cholesky.439), custom_call_target="Cholesky" | custom-call | tf_op jit(solution)/shard_map/jit(cholesky)/cholesky | solution.py:31
  800.7 9.8 custom-call.31
  813.1 11.7 %cholesky.377 = f32[128,128]{1,0:T(8,128)S(1)} custom-call(f32[128,128]{1,0:T(8,128)S(1)} %cholesky.443), custom_call_target="Cholesky" | custom-call | tf_op jit(solution)/shard_map/jit(cholesky)/cholesky | solution.py:31
  826.2 9.9 custom-call.32
  837.7 11.7 %cholesky.398 = f32[128,128]{1,0:T(8,128)S(1)} custom-call(f32[128,128]{1,0:T(8,128)S(1)} %cholesky.448), custom_call_target="Cholesky" | custom-call | tf_op jit(solution)/shard_map/jit(cholesky)/cholesky | solution.py:31
  850.1 9.8 custom-call.33
  861.3 11.7 %cholesky.415 = f32[128,128]{1,0:T(8,128)S(1)} custom-call(f32[128,128]{1,0:T(8,128)S(1)} %convolution_subtract_fusion.10), custom_call_target="Cholesky" | custom-call | tf_op jit(solution)/shard_map/jit(cholesky)/cholesky | solution.py:31
  877.7 11.7 %while.5 = (s32[]{:T(128)}, f32[512,512]{1,0:T(8,128)}, s32[4,2]{0,1:T(2,128)S(1)}, f32[4,128,128]{2,1,0:T(8,128)S(1)}, s32[]{:T(128)}) while((s32[]{:T(128)}, f32[512,512]{1,0:T(8,128)}, s32[4,2]{0,1:T(2,128)S(1)}, f32[4,128,128]{2,1,0:T(8,128)S(1)}, s32[]{:T(128)}) %tuple.72), condition=%wide.while_cond.clone, body=%wide.while_body.clone.sunk | while | flops 2 | bytes 131181 | solution.py:32
  878.4 2.3 bitcast_dynamic-update-slice_fusion.5
  881.4 2.3 bitcast_dynamic-update-slice_fusion.5
  884.3 2.3 bitcast_dynamic-update-slice_fusion.5
  887.2 2.2 bitcast_dynamic-update-slice_fusion.5
  889.4 39.3 %custom-call.34 = f32[4,128,128]{1,2,0:T(8,128)S(1)} custom-call(f32[4,128,128]{2,1,0:T(8,128)S(1)} %get-tuple-element.22), custom_call_target="InvertDiagBlocksLowerTriangular" | custom-call | tf_op jit(solution)/shard_map/jit(_solve_triangular)/triangular_solve | solution.py:32
  930.6 1.5 convolution_subtract_fusion.3
  932.5 1.8 convolution_subtract_fusion.2
  934.5 3.7 convolution_bitcast_fusion
  938.2 97.0 %reduce-scatter.2.cloned.1.call-done = f32[384,512]{0,1:T(8,128)} async-done(((f32[3072,512]{0,1:T(8,128)}), f32[384,512]{0,1:T(8,128)}) %reduce-scatter.2.cloned.1.call-update) | async-done | bytes 786448 | tf_op jit(solution)/shard_map/reduce_scatter | solution.py:34
  (100 shorter events, 37.1 us)
Async XLA Ops:
  6.5 167.9 %copy-start = (bf16[3072,256]{1,0:T(8,128)(2,1)S(1)}, bf16[3072,256]{1,0:T(8,128)(2,1)}, u32[]{:S(2)}) copy-start(bf16[3072,256]{1,0:T(8,128)(2,1)} %param.5) | copy-start | bytes 4718596
  6.5 167.9 %all-gather.4.cloned.1.call-start = ((), (), s32[]{:S(2)}) async-start(), calls=%async_computation.1 | async-start | bytes 14155776 | tf_op jit(solution)/shard_map/all_gather | solution.py:21
  7.3 255.2 %all-gather.6.cloned.1.call-start = ((), (), s32[]{:S(2)}) async-start(), calls=%async_computation.3 | async-start | bytes 4718592 | tf_op jit(solution)/shard_map/all_gather | solution.py:25
  8.0 363.1 %all-reduce.5.cloned.1.call-start = ((), (), s32[]{:S(2)}) async-start(), calls=%async_computation.2 | async-start | bytes 4194304 | tf_op jit(solution)/shard_map/psum | solution.py:22
  182.2 188.8 %copy-start.5 = (f32[256,512]{1,0:T(8,128)S(1)}, f32[256,512]{1,0:T(8,128)}, u32[]{:S(2)}) copy-start(f32[256,512]{1,0:T(8,128)} %param.6) | copy-start | bytes 1572868
  182.3 286.2 %all-reduce.7.cloned.1.call-start = ((), (), s32[]{:S(2)}) async-start(), calls=%async_computation.4 | async-start | bytes 2097152 | tf_op jit(solution)/shard_map/psum | solution.py:30
  379.4 310.0 %all-gather.8.cloned.1.call-start = ((), (), s32[]{:S(2)}) async-start(), calls=%async_computation.5 | async-start | bytes 4718592 | tf_op jit(solution)/shard_map/all_gather | solution.py:25
  468.5 2.7 copy-start.1
  472.6 1.0 copy-start.4
  619.7 164.0 %all-reduce.9.cloned.1.call-start = ((), (), s32[]{:S(2)}) async-start(), calls=%async_computation.6 | async-start | bytes 2097152 | tf_op jit(solution)/shard_map/psum | solution.py:30
  697.9 337.3 %reduce-scatter.2.cloned.1.call-start = ((), (), s32[]{:S(2)}) async-start(), calls=%async_computation.7 | async-start | bytes 7077888 | tf_op jit(solution)/shard_map/reduce_scatter | solution.py:34
  783.7 2.7 copy-start.2
  787.8 1.0 copy-start.3
Sparse Core Ops, SparseCore 0:
  9.5 164.8 all-gather.3
  176.7 70.8 all-gather.5
  250.1 120.8 all-reduce.4
  379.5 88.8 all-reduce.6
  619.8 69.5 all-gather.7
  698.0 85.6 all-reduce.8
  938.4 96.8 reduce-scatter.1
where the time goes:
time: 1050 us; the launch traced here: 1040 us
  waiting for transfers between devices  617 us (59%)
  other arithmetic  246 us (23%)
  blocking collectives  78.1 us (7%)
  matrix products  50.6 us (5%)
  local copies, waits for them, and re-layouts  32.1 us (3%)
  between operations  19.8 us (2%)
    psum x2, waiting for transfers between devices, on_device(): correlation = lax.psum(local_correlation, 'batch')  174 us
    all_gather x1, waiting for transfers between devices, on_device(): lax.all_gather(bases, 'batch', axis=1, tiled=True)  166 us
    another operation x29, other arithmetic, on_device(): factor = jnp.linalg.cholesky(correlation)  158 us
    psum x1, waiting for transfers between devices, on_device(): gram_rows = lax.psum(partial_value, 'rows')  109 us
    reduce_scatter x1, waiting for transfers between devices, on_device(): lax.psum_scatter(jnp.dot(bases, q_low, preferred_element_type=jnp.float32...  97 us
    another operation x5, other arithmetic, on_device(): q_own = jax.scipy.linalg.solve_triangular(factor, lifted.T, lower=True).T  81.3 us
    psum x1, blocking collectives, on_device(): lax.psum(jnp.sum(jnp.square(bases.astype(jnp.float32))), ('rows', 'batch'))  78.1 us
    all_gather x2, waiting for transfers between devices, on_device(): q_full = lax.all_gather(q_own, 'batch', axis=0, tiled=True)  69.7 us
  transfers between devices with their start and end apart: 7, of which 6 were waited for; matrix products, arithmetic and copies ran while one was open for 1% of the time, Pallas kernels for 0%

commit v1 on v0

--- a/solution.py
+++ b/solution.py
@@ -22,7 +22,8 @@
     gram_rows = lax.psum(partial_value, "rows")
     q_own = start
     for iteration in range(ITERS):
-        q_full = lax.all_gather(q_own, "batch", axis=0, tiled=True)
+        outgoing = jnp.stack([q_own] * lax.axis_size("batch"))
+        q_full = jnp.concatenate(lax.all_to_all(outgoing, "batch", 0, 0), axis=0)
         lifted = jnp.dot(gram_rows, q_full, precision=lax.Precision.HIGHEST) / diag_mean + q_own
         local_correlation = lax.dot_general(
             lifted, lifted, (((0,), (0,)), ((), ())), precision=lax.Precision.HIGHEST

time: 1050 us -> 1010 us (0.962)
  waiting for transfers between devices: 617 us -> 532 us
  blocking collectives: 78.1 us -> 114 us
    all_gather x2 -> x0, waiting for transfers between devices: 69.7 us -> none  [on_device(): q_full = lax.all_gather(q_own, 'batch', axis=0, tiled=True)]
    psum x1, waiting for transfers between devices: 109 us -> 55.4 us  [on_device(): gram_rows = lax.psum(partial_value, 'rows')]
    all_to_all x0 -> x1, blocking collectives: none -> 48.7 us  [on_device(): q_full = jnp.concatenate(lax.all_to_all(outgoing, 'batch', 0, 0), axis=0)]
    all_gather x1, waiting for transfers between devices: 166 us -> 205 us  [on_device(): lax.all_gather(bases, 'batch', axis=1, tiled=True)]
    psum x1, blocking collectives: 78.1 us -> 65 us  [on_device(): lax.psum(jnp.sum(jnp.square(bases.astype(jnp.float32))), ('rows', 'batch'))]
  transfers between devices with their start and end apart: 7 -> 6, of which waited for: 6 -> 5; matrix products, arithmetic and copies ran while one was open for 1% -> 1% of each run, Pallas kernels for 0% -> 0%
where the time goes in v1:
time: 1010 us; the launch traced here: 1000 us
  waiting for transfers between devices  532 us (53%)
  other arithmetic  245 us (24%)
  blocking collectives  114 us (11%)
  matrix products  49.8 us (5%)
  local copies, waits for them, and re-layouts  33.2 us (3%)
  between operations  19.4 us (2%)
    all_gather x1, waiting for transfers between devices, on_device(): lax.all_gather(bases, 'batch', axis=1, tiled=True)  205 us
    psum x2, waiting for transfers between devices, on_device(): correlation = lax.psum(local_correlation, 'batch')  174 us
    another operation x29, other arithmetic, on_device(): factor = jnp.linalg.cholesky(correlation)  158 us
    reduce_scatter x1, waiting for transfers between devices, on_device(): lax.psum_scatter(jnp.dot(bases, q_low, preferred_element_type=jnp.float32...  97 us
    another operation x5, other arithmetic, on_device(): q_own = jax.scipy.linalg.solve_triangular(factor, lifted.T, lower=True).T  81.3 us
    psum x1, blocking collectives, on_device(): lax.psum(jnp.sum(jnp.square(bases.astype(jnp.float32))), ('rows', 'batch'))  65 us
    psum x1, waiting for transfers between devices, on_device(): gram_rows = lax.psum(partial_value, 'rows')  55.4 us
    all_to_all x1, blocking collectives, on_device(): q_full = jnp.concatenate(lax.all_to_all(outgoing, 'batch', 0, 0), axis=0)  48.7 us
  transfers between devices with their start and end apart: 6, of which 5 were waited for; matrix products, arithmetic and copies ran while one was open for 1% of the time, Pallas kernels for 0%

profile of v1, /device:TPU:0, one launch (start us, length us, event | category | flops | bytes accessed | tf_op | source)
XLA Modules:
  0.0 1001.9 jit_solution(10805643475178409122)
XLA Ops:
  7.3 3.5 stack.4
  10.8 8.0 all-to-all-start
  18.8 204.9 %all-gather.2.cloned.1.call-done = bf16[3072,2048]{1,0:T(8,128)(2,1)} async-done(((bf16[3072,256]{1,0:T(8,128)(2,1)}), bf16[3072,2048]{1,0:T(8,128)(2,1)}) %all-gather.2.cloned.1.call-update) | async-done | bytes 12582928 | tf_op jit(solution)/shard_map/all_gather | solution.py:21
  223.7 7.8 fusion.76
  233.0 65.0 %psum.29 = f32[]{:T(128)} all-reduce(f32[]{:T(128)} %multiply_reduce_fusion), channel_id=1, replica_groups=mesh['rows'=16,'batch'=8] {'rows','batch'}, use_global_device_ids=true, to_apply=%region_2.0 | all-reduce | flops 1 | bytes 8 | tf_op jit(solution)/shard_map/psum | solution.py:19
  298.7 55.4 %all-reduce.5.cloned.1.call-done = f32[256,2048]{1,0:T(8,128)} async-done(((f32[256,2048]{1,0:T(8,128)}), f32[256,2048]{1,0:T(8,128)}) %all-reduce.5.cloned.1.call-update) | async-done | bytes 2097168 | tf_op jit(solution)/shard_map/psum | solution.py:22
  354.0 6.2 fusion
  360.3 2.0 fusion.77
  362.9 88.5 %all-reduce.7.cloned.1.call-done = f32[512,512]{0,1:T(8,128)} async-done(((f32[512,512]{0,1:T(8,128)}), f32[512,512]{0,1:T(8,128)}) %all-reduce.7.cloned.1.call-update) | async-done | bytes 1048592 | tf_op jit(solution)/shard_map/psum | solution.py:31
  451.4 1.6 copy.4
  455.4 11.7 %cholesky.286 = f32[128,128]{1,0:T(8,128)S(1)} custom-call(f32[128,128]{1,0:T(8,128)S(1)} %cholesky.426), custom_call_target="Cholesky" | custom-call | tf_op jit(solution)/shard_map/jit(cholesky)/cholesky | solution.py:32
  467.1 9.8 custom-call.27
  479.6 11.7 %cholesky.305 = f32[128,128]{1,0:T(8,128)S(1)} custom-call(f32[128,128]{1,0:T(8,128)S(1)} %cholesky.430), custom_call_target="Cholesky" | custom-call | tf_op jit(solution)/shard_map/jit(cholesky)/cholesky | solution.py:32
  491.4 10.0 custom-call.28
  502.9 11.7 %cholesky.326 = f32[128,128]{1,0:T(8,128)S(1)} custom-call(f32[128,128]{1,0:T(8,128)S(1)} %cholesky.435), custom_call_target="Cholesky" | custom-call | tf_op jit(solution)/shard_map/jit(cholesky)/cholesky | solution.py:32
  515.2 9.8 custom-call.29
  526.5 11.7 %cholesky.343 = f32[128,128]{1,0:T(8,128)S(1)} custom-call(f32[128,128]{1,0:T(8,128)S(1)} %convolution_subtract_fusion.11), custom_call_target="Cholesky" | custom-call | tf_op jit(solution)/shard_map/jit(cholesky)/cholesky | solution.py:32
  543.4 11.1 %while.4 = (s32[]{:T(128)}, f32[512,512]{1,0:T(8,128)}, s32[4,2]{0,1:T(2,128)S(1)}, f32[4,128,128]{2,1,0:T(8,128)S(1)}, s32[]{:T(128)}) while((s32[]{:T(128)}, f32[512,512]{1,0:T(8,128)}, s32[4,2]{0,1:T(2,128)S(1)}, f32[4,128,128]{2,1,0:T(8,128)S(1)}, s32[]{:T(128)}) %tuple.52), condition=%wide.while_cond, body=%wide.while_body.sunk | while | flops 2 | bytes 131181 | solution.py:33
  544.0 2.2 bitcast_dynamic-update-slice_fusion.4
  546.8 2.2 bitcast_dynamic-update-slice_fusion.4
  549.6 2.2 bitcast_dynamic-update-slice_fusion.4
  552.3 2.1 bitcast_dynamic-update-slice_fusion.4
  554.4 39.3 %custom-call.30 = f32[4,128,128]{1,2,0:T(8,128)S(1)} custom-call(f32[4,128,128]{2,1,0:T(8,128)S(1)} %get-tuple-element.21), custom_call_target="InvertDiagBlocksLowerTriangular" | custom-call | tf_op jit(solution)/shard_map/jit(_solve_triangular)/triangular_solve | solution.py:33
  595.6 1.5 convolution_subtract_fusion.6
  597.5 1.7 convolution_subtract_fusion.5
  600.4 48.7 %all_to_all.10 = f32[8,256,512]{2,1,0:T(8,128)S(1)} all-to-all(f32[8,256,512]{2,1,0:T(8,128)S(1)} %stack.5), channel_id=1, replica_groups=mesh['rows'=16,'batch'=8] {'batch'}, dimensions={0} | all-to-all | bytes 8388608 | tf_op jit(solution)/shard_map/all_to_all | solution.py:26
  649.1 4.5 bitcast_add_fusion.2
  653.6 2.1 fusion.3
  656.2 85.3 %all-reduce.9.cloned.1.call-done = f32[512,512]{0,1:T(8,128)} async-done(((f32[512,512]{0,1:T(8,128)}), f32[512,512]{0,1:T(8,128)}) %all-reduce.9.cloned.1.call-update) | async-done | bytes 1048592 | tf_op jit(solution)/shard_map/psum | solution.py:31
  741.5 1.6 copy.10
  743.1 1.4 fusion.1
  745.6 11.7 %cholesky.358 = f32[128,128]{1,0:T(8,128)S(1)} custom-call(f32[128,128]{1,0:T(8,128)S(1)} %cholesky.439), custom_call_target="Cholesky" | custom-call | tf_op jit(solution)/shard_map/jit(cholesky)/cholesky | solution.py:32
  757.4 9.8 custom-call.31
  769.8 11.7 %cholesky.377 = f32[128,128]{1,0:T(8,128)S(1)} custom-call(f32[128,128]{1,0:T(8,128)S(1)} %cholesky.443), custom_call_target="Cholesky" | custom-call | tf_op jit(solution)/shard_map/jit(cholesky)/cholesky | solution.py:32
  782.9 10.0 custom-call.32
  794.4 11.7 %cholesky.398 = f32[128,128]{1,0:T(8,128)S(1)} custom-call(f32[128,128]{1,0:T(8,128)S(1)} %cholesky.448), custom_call_target="Cholesky" | custom-call | tf_op jit(solution)/shard_map/jit(cholesky)/cholesky | solution.py:32
  806.8 9.8 custom-call.33
  818.1 11.7 %cholesky.415 = f32[128,128]{1,0:T(8,128)S(1)} custom-call(f32[128,128]{1,0:T(8,128)S(1)} %convolution_subtract_fusion.10), custom_call_target="Cholesky" | custom-call | tf_op jit(solution)/shard_map/jit(cholesky)/cholesky | solution.py:32
  834.4 11.7 %while.5 = (s32[]{:T(128)}, f32[512,512]{1,0:T(8,128)}, s32[4,2]{0,1:T(2,128)S(1)}, f32[4,128,128]{2,1,0:T(8,128)S(1)}, s32[]{:T(128)}) while((s32[]{:T(128)}, f32[512,512]{1,0:T(8,128)}, s32[4,2]{0,1:T(2,128)S(1)}, f32[4,128,128]{2,1,0:T(8,128)S(1)}, s32[]{:T(128)}) %tuple.68), condition=%wide.while_cond.clone, body=%wide.while_body.clone.sunk | while | flops 2 | bytes 131181 | solution.py:33
  835.1 2.3 bitcast_dynamic-update-slice_fusion.5
  838.0 2.3 bitcast_dynamic-update-slice_fusion.5
  840.9 2.3 bitcast_dynamic-update-slice_fusion.5
  843.9 2.2 bitcast_dynamic-update-slice_fusion.5
  846.1 39.3 %custom-call.34 = f32[4,128,128]{1,2,0:T(8,128)S(1)} custom-call(f32[4,128,128]{2,1,0:T(8,128)S(1)} %get-tuple-element.22), custom_call_target="InvertDiagBlocksLowerTriangular" | custom-call | tf_op jit(solution)/shard_map/jit(_solve_triangular)/triangular_solve | solution.py:33
  888.3 1.6 convolution_subtract_fusion.3
  890.2 1.8 convolution_subtract_fusion.2
  892.3 3.7 convolution_bitcast_fusion
  896.0 97.0 %reduce-scatter.2.cloned.1.call-done = f32[384,512]{0,1:T(8,128)} async-done(((f32[3072,512]{0,1:T(8,128)}), f32[384,512]{0,1:T(8,128)}) %reduce-scatter.2.cloned.1.call-update) | async-done | bytes 786448 | tf_op jit(solution)/shard_map/reduce_scatter | solution.py:35
  (97 shorter events, 39.5 us)
Async XLA Ops:
  6.5 217.2 %all-gather.2.cloned.1.call-start = ((), (), s32[]{:S(2)}) async-start(), calls=%async_computation.3 | async-start | bytes 14155776 | tf_op jit(solution)/shard_map/all_gather | solution.py:21
  10.8 212.9 %copy-start = (bf16[3072,256]{1,0:T(8,128)(2,1)S(1)}, bf16[3072,256]{1,0:T(8,128)(2,1)}, u32[]{:S(2)}) copy-start(bf16[3072,256]{1,0:T(8,128)(2,1)} %param.5) | copy-start | bytes 4718596
  10.8 287.9 %all-to-all-start = ((f32[8,256,512]{2,1,0:T(8,128)}), f32[8,256,512]{2,1,0:T(8,128)}, u32[]{:S(2)}, u32[]{:S(2)}) async-start(f32[8,256,512]{2,1,0:T(8,128)} %stack.4), calls=%async_computation | async-start | bytes 8388608 | tf_op jit(solution)/shard_map/all_to_all | solution.py:26
  18.8 335.2 %all-reduce.5.cloned.1.call-start = ((), (), s32[]{:S(2)}) async-start(), calls=%async_computation.4 | async-start | bytes 4194304 | tf_op jit(solution)/shard_map/psum | solution.py:22
  231.5 122.5 %copy-start.4 = (f32[256,512]{1,0:T(8,128)S(1)}, f32[256,512]{1,0:T(8,128)}, u32[]{:S(2)}) copy-start(f32[256,512]{1,0:T(8,128)} %param.6) | copy-start | bytes 1572868
  231.5 219.9 %all-reduce.7.cloned.1.call-start = ((), (), s32[]{:S(2)}) async-start(), calls=%async_computation.5 | async-start | bytes 2097152 | tf_op jit(solution)/shard_map/psum | solution.py:31
  362.3 379.2 %all-reduce.9.cloned.1.call-start = ((), (), s32[]{:S(2)}) async-start(), calls=%async_computation.6 | async-start | bytes 2097152 | tf_op jit(solution)/shard_map/psum | solution.py:31
  454.4 1.0 copy-start.3
  600.4 48.7 %copy-start.1 = (f32[256,2048]{1,0:T(8,128)S(1)}, f32[256,2048]{1,0:T(8,128)}, u32[]{:S(2)}) copy-start(f32[256,2048]{1,0:T(8,128)} %all-reduce.5.cloned.1.call-done) | copy-start | bytes 6291460
  655.7 337.3 %reduce-scatter.2.cloned.1.call-start = ((), (), s32[]{:S(2)}) async-start(), calls=%async_computation.7 | async-start | bytes 7077888 | tf_op jit(solution)/shard_map/reduce_scatter | solution.py:35
  744.5 1.0 copy-start.2
Sparse Core Ops, SparseCore 0:
  9.5 214.1 all-gather.1
  231.6 122.3 all-reduce.4
  362.4 88.8 all-reduce.6
  655.9 85.6 all-reduce.8
  896.1 96.8 reduce-scatter.1
